TPU v7x, 32 devices: a whole 2x2x4 slice. The times are simulated.
32 devices in a mesh: dp: 4 (over y, x), fsdp: 8 (over z, core).
Axes of the slice: x: 2, y: 2, z: 4, core: 2. Of those that a mesh axis runs over, the one named last changes fastest.
Arguments:
- hidden: bfloat16 [2, 4608, 4096], P(None, ('dp', 'fsdp')), may hold values from -120 to 120
- cotangent: bfloat16 [2, 4608, 1024], P(None, ('dp', 'fsdp')), may hold values from -6 to 6
- proj_weight: bfloat16 [2, 4096, 1024], P(None, 'fsdp'), may hold values from -3 to 3
- norm_gain: float32 [2, 4096], replicated, may hold values from 0.1 to 1.9
- prev_factor: bfloat16 [2, 512, 128], replicated, may hold values from -0.25 to 0.25
- factor_ranks: int32 [2, 2], replicated, may hold values from 4 to 64, as said below
- layer_order: int32 [2], replicated, may hold values from 0 to 1, each once
Outputs:
- hidden_grad: bfloat16 [4608, 4096], P(('dp', 'fsdp'))
- basis_factor: float32 [2, 4096, 128], P(None, 'fsdp')
Inputs may be any that keep to these rules, and one draw needn't show every extreme that they name: `factor_ranks`: every draw holds a rank equal to 64 and a rank equal to 4.
All inputs are finite; a program needn't handle non-finite values.
Results may differ from a plain program's by a relative error of at most 0.0056.
Values may be sent and summed in bfloat16 or wider, within the bound.
A program may use at most 64 MiB of HBM per device.

v0:
```python
import math
import jax
import jax.numpy as jnp
from jax import lax
from jax.sharding import PartitionSpec as P

D = 4096


def normalize(hidden_rows, gain_row):
    wide_rows = hidden_rows.astype(jnp.float32)
    inverse = lax.rsqrt(jnp.mean(wide_rows * wide_rows, axis=1, keepdims=True) + 1e-05)
    normed = (wide_rows * inverse * gain_row[None, :]).astype(jnp.bfloat16)
    return (inverse, normed)


def masked_factors(factors, rank_pair):
    rank_cols = factors.shape[1] // 2
    position = jnp.arange(2 * rank_cols)
    column = position % rank_cols
    column_limit = jnp.where(position < rank_cols, rank_pair[0], rank_pair[1])
    return jnp.where((column < column_limit)[None, :], factors, jnp.zeros_like(factors))


def project(grad_rows, kept_factor):
    head_cols = grad_rows.shape[1] // 2
    rank_cols = kept_factor.shape[1] // 2
    keys_part = jnp.dot(
        grad_rows[:, :head_cols], kept_factor[:, :rank_cols], preferred_element_type=jnp.float32
    )
    values_part = jnp.dot(
        grad_rows[:, head_cols:], kept_factor[:, rank_cols:], preferred_element_type=jnp.float32
    )
    return jnp.concatenate([keys_part, values_part], axis=1).astype(jnp.bfloat16)


def gram_pair(factor_shard):
    row_count = factor_shard.shape[0]
    rank_cols = factor_shard.shape[1] // 2
    paired = factor_shard.reshape(row_count, 2, rank_cols)
    return jnp.einsum(
        "rmi,rmj->mij",
        paired,
        paired,
        precision=lax.Precision.HIGHEST,
        preferred_element_type=jnp.float32,
    )


def orthonormal(factor_shard, gram_totals, rank_pair):
    rank_cols = factor_shard.shape[1] // 2
    column = jnp.arange(rank_cols)
    pieces = []
    for member in range(2):
        block_cols = factor_shard[:, member * rank_cols : (member + 1) * rank_cols]
        padded = gram_totals[member] + jnp.diag((column >= rank_pair[member]).astype(jnp.float32))
        lower_factor = jnp.linalg.cholesky(padded)
        pieces.append(
            lax.linalg.triangular_solve(
                lower_factor, block_cols, left_side=False, lower=True, transpose_a=True
            )
        )
    return math.sqrt(D) * jnp.concatenate(pieces, axis=1)


def body(hidden, cotangent, proj_weight, norm_gain, prev_factor, factor_ranks, layer_order):
    layer_count = hidden.shape[0]
    top_slot = layer_order[0]
    inverses = []
    shards = []
    basis_list = []
    for slot_index in range(layer_count):
        inverse, normed = normalize(hidden[slot_index], norm_gain[slot_index])
        inverses.append(inverse)
        kept_factor = masked_factors(prev_factor[slot_index], factor_ranks[slot_index])
        projected = project(cotangent[slot_index], kept_factor)
        local_rows = lax.psum_scatter(
            lax.dot_general(
                normed, projected, (((0,), (0,)), ((), ())), preferred_element_type=jnp.float32
            ),
            "fsdp",
            scatter_dimension=0,
            tiled=True,
        )
        factor_shard = lax.psum(local_rows, "dp")
        shards.append(factor_shard)
    stacked = jnp.stack([gram_pair(factor_shard) for factor_shard in shards])
    all_grams = lax.psum(stacked, "fsdp")
    basis_list = [
        orthonormal(shards[slot_index], all_grams[slot_index], factor_ranks[slot_index])
        for slot_index in range(layer_count)
    ]
    top_grads = lax.dynamic_index_in_dim(cotangent, top_slot, 0, keepdims=False)
    top_weight = lax.dynamic_index_in_dim(proj_weight, top_slot, 0, keepdims=False)
    input_grad = lax.dot_general(
        top_grads,
        lax.all_gather(top_weight, "fsdp", axis=0, tiled=True),
        (((1,), (1,)), ((), ())),
        preferred_element_type=jnp.float32,
    )
    top_inverse = lax.dynamic_index_in_dim(jnp.stack(inverses), top_slot, 0, keepdims=False)
    top_gain = lax.dynamic_index_in_dim(norm_gain, top_slot, 0, keepdims=False)
    top_hidden = lax.dynamic_index_in_dim(hidden, top_slot, 0, keepdims=False).astype(jnp.float32)
    scaled = input_grad * top_gain[None, :]
    unit_rows = top_hidden * top_inverse
    inner_mean = jnp.mean(scaled * unit_rows, axis=1, keepdims=True)
    hidden_grad = (top_inverse * (scaled - unit_rows * inner_mean)).astype(jnp.bfloat16)
    return (hidden_grad, jnp.stack(basis_list))


def solution(mesh):
    in_specs = (
        P(None, ("dp", "fsdp"), None),
        P(None, ("dp", "fsdp"), None),
        P(None, "fsdp", None),
        P(),
        P(),
        P(),
        P(),
    )
    out_specs = (P(("dp", "fsdp"), None), P(None, "fsdp", None))
    return jax.shard_map(body, mesh=mesh, in_specs=in_specs, out_specs=out_specs, check_vma=False)
```

profile of v0, /device:TPU:0, one launch (start us, length us, event | category | flops | bytes accessed | tf_op | source)
XLA Modules:
  0.0 299.6 jit_solution(16446004569142756650)
XLA Ops:
  7.2 1.2 slice_bitcast_fusion.1
  8.5 1.4 fusion.76
  9.9 2.4 fusion.71
  12.3 1.0 bitcast_select_fusion.1
  13.3 0.3 fusion.30
  13.6 0.2 fusion.29
  13.9 2.2 fusion.8
  16.2 3.5 %fusion.17 = f32[4096,128]{1,0:T(8,128)} fusion(f32[4096]{0:T(1024)S(1)} %bitcast.139, f32[144]{0:T(256)S(1)} %add_rsqrt_fusion, bf16[2,144,4096]{2,1,0:T(8,128)(2,1)} %param.10, bf16[144,64]{0,1:T(8,128)(2,1)S(1)} %fusion.30, bf16[144,64]{0,1:T(8,128)(2,1)S(1)} %fusion.29), kind=kOutput, calls=%fused_computation.20 | convolution fusion | flops 153427968 | bytes 3330624 | tf_op jit(solution)/shard_map/dot_general | solution.py:78
  19.8 0.3 fusion.28
  20.3 3.5 %fusion.19 = f32[4096,128]{1,0:T(8,128)} fusion(f32[4096]{0:T(1024)S(1)} %bitcast.138, f32[144]{0:T(256)S(1)} %add_rsqrt_fusion.1, bf16[2,144,4096]{2,1,0:T(8,128)(2,1)} %param.10, bf16[144,64]{0,1:T(8,128)(2,1)S(1)} %fusion.28, bf16[144,64]{0,1:T(8,128)(2,1)S(1)} %fusion.27), kind=kOutput, calls=%fused_computation.21 | convolution fusion | flops 153427968 | bytes 3330624 | tf_op jit(solution)/shard_map/dot_general | solution.py:78
  23.8 34.8 %reduce-scatter.5.cloned.1.call-done = f32[512,128]{1,0:T(8,128)} async-done(((f32[4096,128]{1,0:T(8,128)}), f32[512,128]{1,0:T(8,128)}) %reduce-scatter.5.cloned.1.call-update) | async-done | bytes 262160 | tf_op jit(solution)/shard_map/reduce_scatter | solution.py:77
  58.6 37.0 %reduce-scatter.3.cloned.1.call-done = f32[512,128]{1,0:T(8,128)} async-done(((f32[4096,128]{1,0:T(8,128)}), f32[512,128]{1,0:T(8,128)}) %reduce-scatter.3.cloned.1.call-update) | async-done | bytes 262160 | tf_op jit(solution)/shard_map/reduce_scatter | solution.py:77
  95.6 47.0 %all-reduce.6.cloned.1.call-done = (f32[512,128]{1,0:T(8,128)}, f32[512,128]{1,0:T(8,128)}) async-done(((f32[512,128]{1,0:T(8,128)}, f32[512,128]{1,0:T(8,128)}), (f32[512,128]{1,0:T(8,128)}, f32[512,128]{1,0:T(8,128)})) %all-reduce.6.cloned.1.call-update) | async-done | bytes 524304 | tf_op jit(solution)/shard_map/psum | solution.py:85
  142.7 1.1 copy.22
  143.7 0.4 convolution_bitcast_fusion.4
  144.1 1.1 copy.20
  145.2 0.4 convolution_bitcast_fusion.5
  145.6 0.7 pad_maximum_fusion.1
  146.3 0.2 all-gather.3.cloned.1.call-start
  146.6 1.0 constant_dynamic-slice_fusion.1
  147.6 1.3 compare_convert_fusion.2
  148.9 1.2 compare_convert_fusion
  150.1 51.2 %all-reduce.4.cloned.1.call-done = f32[2,2,64,64]{2,3,1,0:T(8,128)} async-done(((f32[2,2,64,64]{2,3,1,0:T(8,128)}), f32[2,2,64,64]{2,3,1,0:T(8,128)}) %all-reduce.4.cloned.1.call-update) | async-done | bytes 65552 | tf_op jit(solution)/shard_map/psum | solution.py:88
  201.4 0.8 fusion.60
  202.3 5.8 %cholesky.107 = f32[64,64]{1,0:T(8,128)S(1)} custom-call(f32[64,64]{1,0:T(8,128)S(1)} %fusion.62), custom_call_target="Cholesky" | custom-call | tf_op jit(solution)/shard_map/jit(cholesky)/cholesky | solution.py:57
  208.2 0.6 compare_reduce_fusion
  208.8 0.7 fusion.56
  209.5 4.9 %custom-call.11 = f32[1,64,64]{1,2,0:T(8,128)S(1)} custom-call(f32[1,64,64]{2,1,0:T(8,128)S(1)} %fusion.56), custom_call_target="InvertDiagBlocksLowerTriangular" | custom-call | tf_op jit(solution)/shard_map/triangular_solve/custom-call.0 | solution.py:59
  214.5 5.8 %cholesky.96 = f32[64,64]{1,0:T(8,128)S(1)} custom-call(f32[64,64]{1,0:T(8,128)S(1)} %fusion.64), custom_call_target="Cholesky" | custom-call | tf_op jit(solution)/shard_map/jit(cholesky)/cholesky | solution.py:57
  220.4 0.6 compare_reduce_fusion.1
  221.0 0.7 fusion.55
  221.7 4.9 %custom-call.10 = f32[1,64,64]{1,2,0:T(8,128)S(1)} custom-call(f32[1,64,64]{2,1,0:T(8,128)S(1)} %fusion.55), custom_call_target="InvertDiagBlocksLowerTriangular" | custom-call | tf_op jit(solution)/shard_map/triangular_solve/custom-call.0 | solution.py:59
  226.7 5.8 %cholesky.85 = f32[64,64]{1,0:T(8,128)S(1)} custom-call(f32[64,64]{1,0:T(8,128)S(1)} %fusion.66), custom_call_target="Cholesky" | custom-call | tf_op jit(solution)/shard_map/jit(cholesky)/cholesky | solution.py:57
  232.6 0.6 compare_reduce_fusion.2
  233.2 0.7 fusion.54
  233.9 4.9 %custom-call.9 = f32[1,64,64]{1,2,0:T(8,128)S(1)} custom-call(f32[1,64,64]{2,1,0:T(8,128)S(1)} %fusion.54), custom_call_target="InvertDiagBlocksLowerTriangular" | custom-call | tf_op jit(solution)/shard_map/triangular_solve/custom-call.0 | solution.py:59
  238.9 5.8 %cholesky.74 = f32[64,64]{1,0:T(8,128)S(1)} custom-call(f32[64,64]{1,0:T(8,128)S(1)} %fusion.68), custom_call_target="Cholesky" | custom-call | tf_op jit(solution)/shard_map/jit(cholesky)/cholesky | solution.py:57
  244.7 0.6 compare_reduce_fusion.3
  245.4 0.7 fusion.53
  246.1 4.9 %custom-call.8 = f32[1,64,64]{1,2,0:T(8,128)S(1)} custom-call(f32[1,64,64]{2,1,0:T(8,128)S(1)} %fusion.53), custom_call_target="InvertDiagBlocksLowerTriangular" | custom-call | tf_op jit(solution)/shard_map/triangular_solve/custom-call.0 | solution.py:59
  251.0 0.5 convolution_bitcast_fusion
  251.5 0.4 convolution_bitcast_fusion.1
  252.0 0.5 convolution_bitcast_fusion.2
  252.5 0.4 convolution_bitcast_fusion.3
  253.0 1.0 copy.28
  254.0 30.6 %all-gather.3.cloned.1.call-done = bf16[1,4096,1024]{2,1,0:T(8,128)(2,1)} async-done(((bf16[1,512,1024]{2,1,0:T(8,128)(2,1)}), bf16[1,4096,1024]{2,1,0:T(8,128)(2,1)}) %all-gather.3.cloned.1.call-update) | async-done | bytes 8388624 | tf_op jit(solution)/shard_map/all_gather | solution.py:97
  284.6 6.9 %fusion.13 = (f32[144]{0:T(256)S(1)}, f32[144,4096]{1,0:T(8,128)S(1)}) fusion(f32[144]{0:T(256)S(1)} %bitcast.141, bf16[2,144,4096]{2,1,0:T(8,128)(2,1)} %param.10, s32[]{:T(128)S(6)} %select_n.69, f32[4096]{0:T(1024)S(1)} %bitcast.140, bf16[1,4096,1024]{2,1,0:T(8,128)(2,1)} %all-gather.3.cloned.1.call-done, bf16[2,144,1024]{2,1,0:T(8,128)(2,1)S(1)} %copy-done.4), kind=kOutput, calls=%fused_computation.16 | convolution fusion | flops 1210908544 | bytes 12241472 | tf_op jit(solution)/shard_map/dot_general | solution.py:95
  291.5 1.6 fusion.16
  (44 shorter events, 1.2 us)
Async XLA Ops:
  7.2 139.4 %copy-start = (bf16[2,512,1024]{2,1,0:T(8,128)(2,1)S(1)}, bf16[2,512,1024]{2,1,0:T(8,128)(2,1)}, u32[]{:S(2)}) copy-start(bf16[2,512,1024]{2,1,0:T(8,128)(2,1)} %param.12) | copy-start | bytes 6291460
  7.2 6.7 %copy-start.6 = (s32[2]{0:T(128)S(1)}, s32[2]{0:T(128)}, u32[]{:S(2)}) copy-start(s32[2]{0:T(128)} %param.16) | copy-start | bytes 28
  7.2 9.0 %copy-start.5 = (f32[2,4096]{1,0:T(2,128)S(1)}, f32[2,4096]{1,0:T(2,128)}, u32[]{:S(2)}) copy-start(f32[2,4096]{1,0:T(2,128)} %param.13) | copy-start | bytes 98308
  7.2 51.4 %reduce-scatter.5.cloned.1.call-start = ((), (), s32[]{:S(2)}) async-start(), calls=%async_computation.3 | async-start | bytes 2359296 | tf_op jit(solution)/shard_map/reduce_scatter | solution.py:77
  19.7 75.8 %reduce-scatter.3.cloned.1.call-start = ((), (), s32[]{:S(2)}) async-start(), calls=%async_computation.2 | async-start | bytes 2359296 | tf_op jit(solution)/shard_map/reduce_scatter | solution.py:77
  23.8 118.9 %all-reduce.6.cloned.1.call-start = ((), (), s32[]{:S(2)}) async-start(), calls=%async_computation.6 | async-start | bytes 1048576 | tf_op jit(solution)/shard_map/psum | solution.py:85
  95.6 105.8 %all-reduce.4.cloned.1.call-start = ((), (), s32[]{:S(2)}) async-start(), calls=%async_computation.4 | async-start | bytes 262144 | tf_op jit(solution)/shard_map/psum | solution.py:88
  146.3 104.7 %copy-start.3 = (f32[512,128]{1,0:T(8,128)S(1)}, f32[512,128]{1,0:T(8,128)}, u32[]{:S(2)}) copy-start(f32[512,128]{1,0:T(8,128)} %get-tuple-element.10) | copy-start | bytes 786436
  146.3 138.2 %all-gather.3.cloned.1.call-start = ((), (), s32[]{:S(2)}) async-start(), calls=%async_computation.5 | async-start | bytes 9437184 | tf_op jit(solution)/shard_map/all_gather | solution.py:97
  147.6 104.4 %copy-start.2 = (f32[512,128]{1,0:T(8,128)S(1)}, f32[512,128]{1,0:T(8,128)}, u32[]{:S(2)}) copy-start(f32[512,128]{1,0:T(8,128)} %get-tuple-element.11) | copy-start | bytes 786436
  251.0 33.6 %copy-start.4 = (bf16[2,144,1024]{2,1,0:T(8,128)(2,1)S(1)}, bf16[2,144,1024]{2,1,0:T(8,128)(2,1)}, u32[]{:S(2)}) copy-start(bf16[2,144,1024]{2,1,0:T(8,128)(2,1)} %param.11) | copy-start | bytes 1769476
  284.6 6.9 %copy-start.1 = (bf16[2,144,4096]{2,1,0:T(8,128)(2,1)S(1)}, bf16[2,144,4096]{2,1,0:T(8,128)(2,1)}, u32[]{:S(2)}) copy-start(bf16[2,144,4096]{2,1,0:T(8,128)(2,1)} %param.10) | copy-start | bytes 7077892
Sparse Core Ops, SparseCore 0:
  19.9 38.7 reduce-scatter.4
  60.9 34.6 reduce-scatter.2
  98.6 44.0 all-reduce.5
  146.4 54.8 all-reduce.3
  203.4 81.1 all-gather.2
where the time goes:
time: 300 us
  waiting for transfers between devices  201 us (67%)
  other arithmetic  59.6 us (20%)
  matrix products  17.6 us (6%)
  between operations  14.2 us (5%)
  local copies, waits for them, and re-layouts  7.26 us (2%)
    reduce_scatter x2, waiting for transfers between devices, body(): lax.psum_scatter(lax.dot_general(normed, projected, (((0,), (0,)), ((), (...  71.7 us
    psum x1, waiting for transfers between devices, body(): all_grams = lax.psum(stacked, 'fsdp')  51.2 us
    psum x1, waiting for transfers between devices, body(): factor_shard = lax.psum(local_rows, 'dp')  47 us
    all_gather x1, waiting for transfers between devices, body(): lax.all_gather(top_weight, 'fsdp', axis=0, tiled=True)  30.6 us
    another operation x12, other arithmetic, orthonormal(): lower_factor = jnp.linalg.cholesky(padded)  26.1 us
    another operation x8, other arithmetic, orthonormal(): lax.linalg.triangular_solve(lower_factor, block_cols, left_side=False, lo...  22.2 us
    dot_general x2, matrix products, body(): lax.dot_general(normed, projected, (((0,), (0,)), ((), ())), preferred_el...  6.96 us
    dot_general x1, matrix products, body(): lax.dot_general(top_grads, lax.all_gather(top_weight, 'fsdp', axis=0, til...  6.9 us
  transfers between devices with their start and end apart: 5, of which 5 were waited for; matrix products, arithmetic and copies ran while one was open for 20% of the time, Pallas kernels for 0%

commit v1 on v0

--- a/solution.py
+++ b/solution.py
@@ -85,7 +85,11 @@
         factor_shard = lax.psum(local_rows, "dp")
         shards.append(factor_shard)
     stacked = jnp.stack([gram_pair(factor_shard) for factor_shard in shards])
-    all_grams = lax.psum(stacked, "fsdp")
+    all_grams = stacked
+    for hop in (1, 2, 4):
+        all_grams = all_grams + lax.ppermute(
+            all_grams, "fsdp", [(dev, dev ^ hop) for dev in range(8)]
+        )
     basis_list = [
         orthonormal(shards[slot_index], all_grams[slot_index], factor_ranks[slot_index])
         for slot_index in range(layer_count)

time: 300 us -> 247 us (0.82)
  waiting for transfers between devices: 201 us -> 144 us
  starting transfers between devices: 0.38 us -> 4.45 us
    psum x1 -> x0, waiting for transfers between devices: 51.2 us -> none  [body(): all_grams = lax.psum(stacked, 'fsdp')]
    all_gather x1, waiting for transfers between devices: 30.6 us -> 9.06 us  [body(): lax.all_gather(top_weight, 'fsdp', axis=0, tiled=True)]
    ppermute x0 -> x3, waiting for transfers between devices: none -> 17.9 us  [body(): lax.ppermute(all_grams, 'fsdp', [(dev, dev ^ hop) for dev in range(8)])]
    ppermute x0 -> x3, starting transfers between devices: none -> 4.1 us  [body(): lax.ppermute(all_grams, 'fsdp', [(dev, dev ^ hop) for dev in range(8)])]
  transfers between devices with their start and end apart: 5 -> 7, of which waited for: 5 -> 7; matrix products, arithmetic and copies ran while one was open for 20% -> 25% of each run, Pallas kernels for 0% -> 0%
where the time goes in v1:
time: 247 us
  waiting for transfers between devices  144 us (58%)
  other arithmetic  58.4 us (24%)
  matrix products  17.6 us (7%)
  between operations  14.2 us (6%)
  local copies, waits for them, and re-layouts  7.37 us (3%)
  starting transfers between devices  4.45 us (2%)
    reduce_scatter x2, waiting for transfers between devices, body(): lax.psum_scatter(lax.dot_general(normed, projected, (((0,), (0,)), ((), (...  71.7 us
    psum x1, waiting for transfers between devices, body(): factor_shard = lax.psum(local_rows, 'dp')  45.8 us
    another operation x12, other arithmetic, orthonormal(): lower_factor = jnp.linalg.cholesky(padded)  26.1 us
    another operation x8, other arithmetic, orthonormal(): lax.linalg.triangular_solve(lower_factor, block_cols, left_side=False, lo...  22.2 us
    ppermute x3, waiting for transfers between devices, body(): lax.ppermute(all_grams, 'fsdp', [(dev, dev ^ hop) for dev in range(8)])  17.9 us
    all_gather x1, waiting for transfers between devices, body(): lax.all_gather(top_weight, 'fsdp', axis=0, tiled=True)  9.06 us
    dot_general x2, matrix products, body(): lax.dot_general(normed, projected, (((0,), (0,)), ((), ())), preferred_el...  6.96 us
    dot_general x1, matrix products, body(): lax.dot_general(top_grads, lax.all_gather(top_weight, 'fsdp', axis=0, til...  6.9 us
  transfers between devices with their start and end apart: 7, of which 7 were waited for; matrix products, arithmetic and copies ran while one was open for 25% of the time, Pallas kernels for 0%

profile of v1, /device:TPU:0, one launch (start us, length us, event | category | flops | bytes accessed | tf_op | source)
XLA Modules:
  0.0 246.5 jit_solution(13303343819824546037)
XLA Ops:
  7.2 1.2 slice_bitcast_fusion.1
  8.5 1.5 fusion.77
  10.0 2.6 %fusion.71 = (pred[128]{0:T(512)(128)(4,1)S(1)}, pred[128]{0:T(512)(128)(4,1)S(1)}) fusion(s32[]{:T(128)} %bitcast.13, s32[]{:T(128)} %bitcast.12, s32[]{:T(128)} %bitcast.23, s32[]{:T(128)} %bitcast.22), kind=kLoop, calls=%fused_computation.126 | loop fusion | flops 1408 | bytes 272 | tf_op jit(solution)/shard_map/lt | solution.py:22
  12.6 1.0 bitcast_select_fusion.1
  13.6 0.3 fusion.30
  14.1 2.2 fusion.8
  16.4 3.5 %fusion.17 = f32[4096,128]{1,0:T(8,128)} fusion(f32[4096]{0:T(1024)S(1)} %bitcast.139, f32[144]{0:T(256)S(1)} %add_rsqrt_fusion, bf16[2,144,4096]{2,1,0:T(8,128)(2,1)} %param.10, bf16[144,64]{0,1:T(8,128)(2,1)S(1)} %fusion.30, bf16[144,64]{0,1:T(8,128)(2,1)S(1)} %fusion.29), kind=kOutput, calls=%fused_computation.20 | convolution fusion | flops 153427968 | bytes 3330624 | tf_op jit(solution)/shard_map/dot_general | solution.py:78
  20.0 0.3 fusion.28
  20.5 3.5 %fusion.19 = f32[4096,128]{1,0:T(8,128)} fusion(f32[4096]{0:T(1024)S(1)} %bitcast.138, f32[144]{0:T(256)S(1)} %add_rsqrt_fusion.1, bf16[2,144,4096]{2,1,0:T(8,128)(2,1)} %param.10, bf16[144,64]{0,1:T(8,128)(2,1)S(1)} %fusion.28, bf16[144,64]{0,1:T(8,128)(2,1)S(1)} %fusion.27), kind=kOutput, calls=%fused_computation.21 | convolution fusion | flops 153427968 | bytes 3330624 | tf_op jit(solution)/shard_map/dot_general | solution.py:78
  24.1 34.8 %reduce-scatter.5.cloned.1.call-done = f32[512,128]{1,0:T(8,128)} async-done(((f32[4096,128]{1,0:T(8,128)}), f32[512,128]{1,0:T(8,128)}) %reduce-scatter.5.cloned.1.call-update) | async-done | bytes 262160 | tf_op jit(solution)/shard_map/reduce_scatter | solution.py:77
  58.8 36.9 %reduce-scatter.3.cloned.1.call-done = f32[512,128]{1,0:T(8,128)} async-done(((f32[4096,128]{1,0:T(8,128)}), f32[512,128]{1,0:T(8,128)}) %reduce-scatter.3.cloned.1.call-update) | async-done | bytes 262160 | tf_op jit(solution)/shard_map/reduce_scatter | solution.py:77
  95.8 0.2 all-gather.3.cloned.1.call-start
  96.0 1.0 constant_dynamic-slice_fusion.1
  97.1 45.8 %all-reduce.3.cloned.1.call-done = (f32[512,128]{1,0:T(8,128)}, f32[512,128]{1,0:T(8,128)}) async-done(((f32[512,128]{1,0:T(8,128)}, f32[512,128]{1,0:T(8,128)}), (f32[512,128]{1,0:T(8,128)}, f32[512,128]{1,0:T(8,128)})) %all-reduce.3.cloned.1.call-update) | async-done | bytes 524304 | tf_op jit(solution)/shard_map/psum | solution.py:85
  142.8 1.1 copy.22
  143.9 1.1 copy.20
  145.0 0.4 convolution_bitcast_fusion.4
  145.5 0.4 convolution_bitcast_fusion.5
  146.0 1.3 compare_convert_fusion.2
  147.3 1.6 collective-permute-start.1
  148.9 1.3 compare_convert_fusion
  150.2 3.1 %collective-permute-done.1 = f32[2,2,64,64]{2,3,1,0:T(8,128)S(1)} collective-permute-done((f32[2,2,64,64]{2,3,1,0:T(8,128)S(1)}, f32[2,2,64,64]{2,3,1,0:T(8,128)S(1)}, u32[]{:S(2)}, u32[]{:S(2)}) %collective-permute-start.1) | collective-permute-done | bytes 65568 | tf_op jit(solution)/shard_map/ppermute | solution.py:90
  153.3 2.5 %collective-permute-start.2 = (f32[2,2,64,64]{2,3,1,0:T(8,128)S(1)}, f32[2,2,64,64]{2,3,1,0:T(8,128)S(1)}, u32[]{:S(2)}, u32[]{:S(2)}) collective-permute-start(f32[2,2,64,64]{2,3,1,0:T(8,128)S(1)} %fusion.82), channel_id=1, source_target_pairs={{0,4},{1,5},{2,6},{3,7},{4,0},{5,1},{6,2},{7,3},{8,12},{9,13},{10,... | collective-permute-start | bytes 196616 | tf_op jit(solution)/shard_map/ppermute | solution.py:90
  155.8 14.8 %collective-permute-done.2 = f32[2,2,64,64]{2,3,1,0:T(8,128)S(1)} collective-permute-done((f32[2,2,64,64]{2,3,1,0:T(8,128)S(1)}, f32[2,2,64,64]{2,3,1,0:T(8,128)S(1)}, u32[]{:S(2)}, u32[]{:S(2)}) %collective-permute-start.2) | collective-permute-done | bytes 65568 | tf_op jit(solution)/shard_map/ppermute | solution.py:90
  170.7 5.8 %cholesky.107 = f32[64,64]{1,0:T(8,128)S(1)} custom-call(f32[64,64]{1,0:T(8,128)S(1)} %fusion.62), custom_call_target="Cholesky" | custom-call | tf_op jit(solution)/shard_map/jit(cholesky)/cholesky | solution.py:57
  176.6 0.6 compare_reduce_fusion
  177.2 0.7 fusion.56
  177.9 4.9 %custom-call.11 = f32[1,64,64]{1,2,0:T(8,128)S(1)} custom-call(f32[1,64,64]{2,1,0:T(8,128)S(1)} %fusion.56), custom_call_target="InvertDiagBlocksLowerTriangular" | custom-call | tf_op jit(solution)/shard_map/triangular_solve/custom-call.0 | solution.py:59
  182.9 5.8 %cholesky.96 = f32[64,64]{1,0:T(8,128)S(1)} custom-call(f32[64,64]{1,0:T(8,128)S(1)} %fusion.64), custom_call_target="Cholesky" | custom-call | tf_op jit(solution)/shard_map/jit(cholesky)/cholesky | solution.py:57
  188.8 0.6 compare_reduce_fusion.1
  189.4 0.7 fusion.55
  190.1 4.9 %custom-call.10 = f32[1,64,64]{1,2,0:T(8,128)S(1)} custom-call(f32[1,64,64]{2,1,0:T(8,128)S(1)} %fusion.55), custom_call_target="InvertDiagBlocksLowerTriangular" | custom-call | tf_op jit(solution)/shard_map/triangular_solve/custom-call.0 | solution.py:59
  195.1 5.8 %cholesky.85 = f32[64,64]{1,0:T(8,128)S(1)} custom-call(f32[64,64]{1,0:T(8,128)S(1)} %fusion.66), custom_call_target="Cholesky" | custom-call | tf_op jit(solution)/shard_map/jit(cholesky)/cholesky | solution.py:57
  201.0 0.6 compare_reduce_fusion.2
  201.6 0.7 fusion.54
  202.3 4.9 %custom-call.9 = f32[1,64,64]{1,2,0:T(8,128)S(1)} custom-call(f32[1,64,64]{2,1,0:T(8,128)S(1)} %fusion.54), custom_call_target="InvertDiagBlocksLowerTriangular" | custom-call | tf_op jit(solution)/shard_map/triangular_solve/custom-call.0 | solution.py:59
  207.3 5.8 %cholesky.74 = f32[64,64]{1,0:T(8,128)S(1)} custom-call(f32[64,64]{1,0:T(8,128)S(1)} %fusion.68), custom_call_target="Cholesky" | custom-call | tf_op jit(solution)/shard_map/jit(cholesky)/cholesky | solution.py:57
  213.2 0.6 compare_reduce_fusion.3
  213.8 0.7 fusion.53
  214.5 4.9 %custom-call.8 = f32[1,64,64]{1,2,0:T(8,128)S(1)} custom-call(f32[1,64,64]{2,1,0:T(8,128)S(1)} %fusion.53), custom_call_target="InvertDiagBlocksLowerTriangular" | custom-call | tf_op jit(solution)/shard_map/triangular_solve/custom-call.0 | solution.py:59
  219.4 0.5 convolution_bitcast_fusion
  219.9 0.4 convolution_bitcast_fusion.1
  220.4 0.5 convolution_bitcast_fusion.2
  220.9 0.4 convolution_bitcast_fusion.3
  221.4 1.0 copy.28
  222.4 9.1 %all-gather.3.cloned.1.call-done = bf16[1,4096,1024]{2,1,0:T(8,128)(2,1)} async-done(((bf16[1,512,1024]{2,1,0:T(8,128)(2,1)}), bf16[1,4096,1024]{2,1,0:T(8,128)(2,1)}) %all-gather.3.cloned.1.call-update) | async-done | bytes 8388624 | tf_op jit(solution)/shard_map/all_gather | solution.py:101
  231.5 6.9 %fusion.13 = (f32[144]{0:T(256)S(1)}, f32[144,4096]{1,0:T(8,128)S(1)}) fusion(f32[144]{0:T(256)S(1)} %bitcast.141, bf16[2,144,4096]{2,1,0:T(8,128)(2,1)} %param.10, s32[]{:T(128)S(6)} %select_n.69, f32[4096]{0:T(1024)S(1)} %bitcast.140, bf16[1,4096,1024]{2,1,0:T(8,128)(2,1)} %all-gather.3.cloned.1.call-done, bf16[2,144,1024]{2,1,0:T(8,128)(2,1)S(1)} %copy-done.4), kind=kOutput, calls=%fused_computation.16 | convolution fusion | flops 1210908544 | bytes 12241472 | tf_op jit(solution)/shard_map/dot_general | solution.py:99
  238.4 1.6 fusion.16
  (50 shorter events, 1.5 us)
Async XLA Ops:
  7.2 88.8 %copy-start = (bf16[2,512,1024]{2,1,0:T(8,128)(2,1)S(1)}, bf16[2,512,1024]{2,1,0:T(8,128)(2,1)}, u32[]{:S(2)}) copy-start(bf16[2,512,1024]{2,1,0:T(8,128)(2,1)} %param.12) | copy-start | bytes 6291460
  7.2 6.9 %copy-start.6 = (s32[2]{0:T(128)S(1)}, s32[2]{0:T(128)}, u32[]{:S(2)}) copy-start(s32[2]{0:T(128)} %param.16) | copy-start | bytes 28
  7.2 9.2 %copy-start.5 = (f32[2,4096]{1,0:T(2,128)S(1)}, f32[2,4096]{1,0:T(2,128)}, u32[]{:S(2)}) copy-start(f32[2,4096]{1,0:T(2,128)} %param.13) | copy-start | bytes 98308
  7.2 51.6 %reduce-scatter.5.cloned.1.call-start = ((), (), s32[]{:S(2)}) async-start(), calls=%async_computation.3 | async-start | bytes 2359296 | tf_op jit(solution)/shard_map/reduce_scatter | solution.py:77
  20.0 75.8 %reduce-scatter.3.cloned.1.call-start = ((), (), s32[]{:S(2)}) async-start(), calls=%async_computation.2 | async-start | bytes 2359296 | tf_op jit(solution)/shard_map/reduce_scatter | solution.py:77
  24.0 118.8 %all-reduce.3.cloned.1.call-start = ((), (), s32[]{:S(2)}) async-start(), calls=%async_computation.5 | async-start | bytes 1048576 | tf_op jit(solution)/shard_map/psum | solution.py:85
  95.8 135.7 %all-gather.3.cloned.1.call-start = ((), (), s32[]{:S(2)}) async-start(), calls=%async_computation.4 | async-start | bytes 9437184 | tf_op jit(solution)/shard_map/all_gather | solution.py:101
  143.9 75.5 %copy-start.3 = (f32[512,128]{1,0:T(8,128)S(1)}, f32[512,128]{1,0:T(8,128)}, u32[]{:S(2)}) copy-start(f32[512,128]{1,0:T(8,128)} %get-tuple-element.10) | copy-start | bytes 786436
  145.4 74.9 %copy-start.2 = (f32[512,128]{1,0:T(8,128)S(1)}, f32[512,128]{1,0:T(8,128)}, u32[]{:S(2)}) copy-start(f32[512,128]{1,0:T(8,128)} %get-tuple-element.11) | copy-start | bytes 786436
  145.9 1.4 collective-permute-start
  147.3 5.9 %collective-permute-start.1 = (f32[2,2,64,64]{2,3,1,0:T(8,128)S(1)}, f32[2,2,64,64]{2,3,1,0:T(8,128)S(1)}, u32[]{:S(2)}, u32[]{:S(2)}) collective-permute-start(f32[2,2,64,64]{2,3,1,0:T(8,128)S(1)} %fusion.75), channel_id=1, source_target_pairs={{0,2},{1,3},{2,0},{3,1},{4,6},{5,7},{6,4},{7,5},{8,10},{9,11},{10,... | collective-permute-start | bytes 196616 | tf_op jit(solution)/shard_map/ppermute | solution.py:90
  153.3 17.3 %collective-permute-start.2 = (f32[2,2,64,64]{2,3,1,0:T(8,128)S(1)}, f32[2,2,64,64]{2,3,1,0:T(8,128)S(1)}, u32[]{:S(2)}, u32[]{:S(2)}) collective-permute-start(f32[2,2,64,64]{2,3,1,0:T(8,128)S(1)} %fusion.82), channel_id=1, source_target_pairs={{0,4},{1,5},{2,6},{3,7},{4,0},{5,1},{6,2},{7,3},{8,12},{9,13},{10,... | collective-permute-start | bytes 196616 | tf_op jit(solution)/shard_map/ppermute | solution.py:90
  219.4 12.1 %copy-start.4 = (bf16[2,144,1024]{2,1,0:T(8,128)(2,1)S(1)}, bf16[2,144,1024]{2,1,0:T(8,128)(2,1)}, u32[]{:S(2)}) copy-start(bf16[2,144,1024]{2,1,0:T(8,128)(2,1)} %param.11) | copy-start | bytes 1769476
  231.5 6.9 %copy-start.1 = (bf16[2,144,4096]{2,1,0:T(8,128)(2,1)S(1)}, bf16[2,144,4096]{2,1,0:T(8,128)(2,1)}, u32[]{:S(2)}) copy-start(bf16[2,144,4096]{2,1,0:T(8,128)(2,1)} %param.10) | copy-start | bytes 7077892
Sparse Core Ops, SparseCore 0:
  20.1 38.6 reduce-scatter.4
  61.1 34.5 reduce-scatter.2
  98.7 44.0 all-reduce.2
  144.9 86.5 all-gather.2
